TPU v7x, 256 devices: a whole 4x4x8 slice. The times are simulated.
256 devices in a mesh: row: 8 (over z), col: 32 (over y, x, core).
Axes of the slice: x: 4, y: 4, z: 8, core: 2. Of those that a mesh axis runs over, the one named last changes fastest.
Arguments:
- factor: bfloat16 [32, 8, 8, 32, 128, 128], P(None, 'row', None, 'col'), may hold values from -0.046875 to 0.046875
- pattern: int32 [32, 8, 8, 32], P(None, 'row', None, 'col'), may hold values 0 or 1
- loads: float32 [8, 32, 128, 256], P(None, 'col'), may hold values from -6 to 6
- block_inverse: float32 [8, 32, 128, 128], P(None, 'col'), may hold values from -1 to 2, as said below
Outputs:
- solution: float32 [8, 32, 128, 256], P(None, 'col')
Inputs may be any that keep to these rules, and one draw needn't show every extreme that they name: `block_inverse`: each block is lower triangular with diagonal entries between 0.5 and 1.5.
All inputs are finite; a program needn't handle non-finite values. No bound on the sum of `pattern` on one device may be relied on, other than what follows from the above.
Results may differ from a plain program's by a relative error of at most 0.0045.
Values may be sent and summed in bfloat16 or wider, within the bound.
No kernel may reach another device: no remote copies, remote signals or barrier semaphores. Data moves between devices by JAX's collectives and lax.ppermute only.
A program may use at most 128 MiB of HBM per device.

v0:
```python
import jax
import jax.numpy as jnp
from jax import lax
from jax.sharding import PartitionSpec as P

LEVELS = 8


def spread(value, axis, source):
    kept = jnp.where(lax.axis_index(axis) == source, value, 0).astype(value.dtype)
    return lax.psum(kept, axis)


def per_device(factor, pattern, loads, block_inverse):
    row_count = lax.axis_size("row")
    col_count = lax.axis_size("col")
    groups = col_count // row_count
    my_row = lax.axis_index("row")
    my_col = lax.axis_index("col")
    masked = factor[:, 0, :, 0] * pattern[:, 0, :, 0].astype(jnp.bfloat16)[:, :, None, None]
    per_row = factor.shape[0] // LEVELS
    per_col = factor.shape[2] // LEVELS
    rhs_local = loads[:, 0]
    inverse_local = block_inverse[:, 0]
    forward_vals = []
    forward_low = []
    for level_id in range(LEVELS):
        rhs_level = rhs_local[level_id * per_col : (level_id + 1) * per_col]
        inverse_level = inverse_local[level_id * per_col : (level_id + 1) * per_col]
        if level_id > 0:
            panel = masked[level_id * per_row : (level_id + 1) * per_row, : level_id * per_col]
            earlier = jnp.concatenate(forward_low, axis=0)
            partial_sum = jnp.einsum(
                "abpq,bqs->aps", panel, earlier, preferred_element_type=jnp.float32
            )
            row_total = lax.psum(partial_sum, "col")
            row_total = row_total.reshape((per_col, groups) + row_total.shape[1:])
            own_total = lax.dynamic_index_in_dim(
                row_total, my_col // row_count, axis=1, keepdims=False
            )
            solved = jnp.einsum(
                "mpq,mqs->mps",
                inverse_level,
                rhs_level - own_total,
                precision=lax.Precision.HIGHEST,
            )
            solved = spread(solved, "row", my_col % row_count)
        else:
            solved = jnp.einsum(
                "mpq,mqs->mps", inverse_level, rhs_level, precision=lax.Precision.HIGHEST
            )
        forward_vals.append(solved)
        forward_low.append(solved.astype(jnp.bfloat16))
    solution_parts = [None] * LEVELS
    later = []
    for level_id in reversed(range(LEVELS)):
        inverse_level = inverse_local[level_id * per_col : (level_id + 1) * per_col]
        resid = forward_vals[level_id]
        if level_id < LEVELS - 1:
            panel = masked[
                (level_id + 1) * per_row :, level_id * per_col : (level_id + 1) * per_col
            ]
            after = jnp.concatenate(later, axis=0)
            partial_sum = jnp.einsum(
                "abpq,aps->bqs", panel, after, preferred_element_type=jnp.float32
            )
            resid = resid - lax.psum(partial_sum, "row")
        solved = jnp.einsum("mqp,mqs->mps", inverse_level, resid, precision=lax.Precision.HIGHEST)
        solution_parts[level_id] = solved
        if level_id > 0:
            low_solved = solved.astype(jnp.bfloat16)
            pieces = lax.all_gather(low_solved[None], "col", axis=0, tiled=True)
            pieces = pieces.reshape((groups, row_count) + low_solved.shape)
            picked = lax.dynamic_index_in_dim(pieces, my_row, axis=1, keepdims=False)
            arranged = jnp.swapaxes(picked, 0, 1).reshape((per_row,) + low_solved.shape[1:])
            later = [arranged] + later
    solution = jnp.concatenate(solution_parts, axis=0)
    return solution[:, None]


def solution(mesh):
    in_specs = (
        P(None, "row", None, "col", None, None),
        P(None, "row", None, "col"),
        P(None, "col", None, None),
        P(None, "col", None, None),
    )
    out_specs = P(None, "col", None, None)
    return jax.shard_map(
        per_device, mesh=mesh, in_specs=in_specs, out_specs=out_specs, check_vma=False
    )
```

profile of v0, /device:TPU:2, one launch (start us, length us, event | category | flops | bytes accessed | tf_op | source)
XLA Modules:
  0.0 2246.1 jit_solution(3896068341786399089)
XLA Ops:
  8.5 7.4 bitcast_multiply_fusion
  15.9 1.9 fusion.36
  17.9 116.1 %all-reduce.22.cloned.1.call-done = f32[4,128,256]{2,1,0:T(8,128)} async-done(((f32[4,128,256]{2,1,0:T(8,128)}), f32[4,128,256]{2,1,0:T(8,128)}) %all-reduce.22.cloned.1.call-update) | async-done | bytes 524304 | tf_op jit(solution)/shard_map/psum | solution.py:36
  134.0 1.8 fusion.7
  135.9 72.4 %all-reduce.24.cloned.1.call-done = f32[1,128,256]{2,1,0:T(8,128)} async-done(((f32[1,128,256]{2,1,0:T(8,128)}), f32[1,128,256]{2,1,0:T(8,128)}) %all-reduce.24.cloned.1.call-update) | async-done | bytes 131088 | tf_op jit(solution)/shard_map/psum | solution.py:11
  209.3 2.0 convolution_bitcast_fusion.5
  211.3 111.8 %all-reduce.26.cloned.1.call-done = f32[4,128,256]{2,1,0:T(8,128)} async-done(((f32[4,128,256]{2,1,0:T(8,128)}), f32[4,128,256]{2,1,0:T(8,128)}) %all-reduce.26.cloned.1.call-update) | async-done | bytes 524304 | tf_op jit(solution)/shard_map/psum | solution.py:36
  323.1 1.8 fusion.6
  325.1 72.3 %all-reduce.28.cloned.1.call-done = f32[1,128,256]{2,1,0:T(8,128)} async-done(((f32[1,128,256]{2,1,0:T(8,128)}), f32[1,128,256]{2,1,0:T(8,128)}) %all-reduce.28.cloned.1.call-update) | async-done | bytes 131088 | tf_op jit(solution)/shard_map/psum | solution.py:11
  398.3 2.1 convolution_bitcast_fusion.4
  400.5 111.6 %all-reduce.30.cloned.1.call-done = f32[4,128,256]{2,1,0:T(8,128)} async-done(((f32[4,128,256]{2,1,0:T(8,128)}), f32[4,128,256]{2,1,0:T(8,128)}) %all-reduce.30.cloned.1.call-update) | async-done | bytes 524304 | tf_op jit(solution)/shard_map/psum | solution.py:36
  512.1 1.8 fusion.5
  514.0 72.3 %all-reduce.32.cloned.1.call-done = f32[1,128,256]{2,1,0:T(8,128)} async-done(((f32[1,128,256]{2,1,0:T(8,128)}), f32[1,128,256]{2,1,0:T(8,128)}) %all-reduce.32.cloned.1.call-update) | async-done | bytes 131088 | tf_op jit(solution)/shard_map/psum | solution.py:11
  587.3 2.1 convolution_bitcast_fusion.3
  589.5 111.6 %all-reduce.34.cloned.1.call-done = f32[4,128,256]{2,1,0:T(8,128)} async-done(((f32[4,128,256]{2,1,0:T(8,128)}), f32[4,128,256]{2,1,0:T(8,128)}) %all-reduce.34.cloned.1.call-update) | async-done | bytes 524304 | tf_op jit(solution)/shard_map/psum | solution.py:36
  701.1 1.8 fusion.4
  703.1 72.4 %all-reduce.36.cloned.1.call-done = f32[1,128,256]{2,1,0:T(8,128)} async-done(((f32[1,128,256]{2,1,0:T(8,128)}), f32[1,128,256]{2,1,0:T(8,128)}) %all-reduce.36.cloned.1.call-update) | async-done | bytes 131088 | tf_op jit(solution)/shard_map/psum | solution.py:11
  776.4 2.3 convolution_bitcast_fusion.2
  778.8 111.6 %all-reduce.38.cloned.1.call-done = f32[4,128,256]{2,1,0:T(8,128)} async-done(((f32[4,128,256]{2,1,0:T(8,128)}), f32[4,128,256]{2,1,0:T(8,128)}) %all-reduce.38.cloned.1.call-update) | async-done | bytes 524304 | tf_op jit(solution)/shard_map/psum | solution.py:36
  890.4 1.8 fusion.3
  892.3 72.3 %all-reduce.40.cloned.1.call-done = f32[1,128,256]{2,1,0:T(8,128)} async-done(((f32[1,128,256]{2,1,0:T(8,128)}), f32[1,128,256]{2,1,0:T(8,128)}) %all-reduce.40.cloned.1.call-update) | async-done | bytes 131088 | tf_op jit(solution)/shard_map/psum | solution.py:11
  965.6 2.3 convolution_bitcast_fusion.1
  967.9 111.7 %all-reduce.42.cloned.1.call-done = f32[4,128,256]{2,1,0:T(8,128)} async-done(((f32[4,128,256]{2,1,0:T(8,128)}), f32[4,128,256]{2,1,0:T(8,128)}) %all-reduce.42.cloned.1.call-update) | async-done | bytes 524304 | tf_op jit(solution)/shard_map/psum | solution.py:36
  1079.6 1.8 fusion.2
  1081.5 72.3 %all-reduce.44.cloned.1.call-done = f32[1,128,256]{2,1,0:T(8,128)} async-done(((f32[1,128,256]{2,1,0:T(8,128)}), f32[1,128,256]{2,1,0:T(8,128)}) %all-reduce.44.cloned.1.call-update) | async-done | bytes 131088 | tf_op jit(solution)/shard_map/psum | solution.py:11
  1154.8 2.4 convolution_bitcast_fusion
  1157.2 111.7 %all-reduce.46.cloned.1.call-done = f32[4,128,256]{2,1,0:T(8,128)} async-done(((f32[4,128,256]{2,1,0:T(8,128)}), f32[4,128,256]{2,1,0:T(8,128)}) %all-reduce.46.cloned.1.call-update) | async-done | bytes 524304 | tf_op jit(solution)/shard_map/psum | solution.py:36
  1268.9 1.8 fusion.1
  1270.8 72.3 %all-reduce.48.cloned.1.call-done = f32[128,256]{1,0:T(8,128)} async-done(((f32[128,256]{1,0:T(8,128)}), f32[128,256]{1,0:T(8,128)}) %all-reduce.48.cloned.1.call-update) | async-done | bytes 131088 | tf_op jit(solution)/shard_map/psum | solution.py:11
  1343.2 1.9 bitcast_convert_fusion.6
  1345.2 48.3 %all-gather.15.cloned.1.call-done = bf16[4096,256]{0,1:T(8,128)(2,1)} async-done(((bf16[128,256]{0,1:T(8,128)(2,1)}), bf16[4096,256]{0,1:T(8,128)(2,1)}) %all-gather.15.cloned.1.call-update) | async-done | bytes 2097168 | tf_op jit(solution)/shard_map/all_gather | solution.py:72
  1393.4 2.1 copy.59
  1396.6 1.8 convolution_bitcast_fusion.9
  1398.4 71.8 %all-reduce.50.cloned.1.call-done = f32[1,128,256]{2,1,0:T(8,128)} async-done(((f32[1,128,256]{2,1,0:T(8,128)}), f32[1,128,256]{2,1,0:T(8,128)}) %all-reduce.50.cloned.1.call-update) | async-done | bytes 131088 | tf_op jit(solution)/shard_map/psum | solution.py:67
  1470.2 1.9 bitcast_convert_fusion.5
  1472.2 48.6 %all-gather.17.cloned.1.call-done = bf16[4096,256]{0,1:T(8,128)(2,1)} async-done(((bf16[128,256]{0,1:T(8,128)(2,1)}), bf16[4096,256]{0,1:T(8,128)(2,1)}) %all-gather.17.cloned.1.call-update) | async-done | bytes 2097168 | tf_op jit(solution)/shard_map/all_gather | solution.py:72
  1520.8 2.1 copy.60
  1523.9 1.9 convolution_bitcast_fusion.8
  1525.9 71.8 %all-reduce.52.cloned.1.call-done = f32[1,128,256]{2,1,0:T(8,128)} async-done(((f32[1,128,256]{2,1,0:T(8,128)}), f32[1,128,256]{2,1,0:T(8,128)}) %all-reduce.52.cloned.1.call-update) | async-done | bytes 131088 | tf_op jit(solution)/shard_map/psum | solution.py:67
  1597.6 1.9 bitcast_convert_fusion.4
  1599.6 48.4 %all-gather.19.cloned.1.call-done = bf16[4096,256]{0,1:T(8,128)(2,1)} async-done(((bf16[128,256]{0,1:T(8,128)(2,1)}), bf16[4096,256]{0,1:T(8,128)(2,1)}) %all-gather.19.cloned.1.call-update) | async-done | bytes 2097168 | tf_op jit(solution)/shard_map/all_gather | solution.py:72
  1648.1 2.1 copy.61
  1651.2 2.0 convolution_bitcast_fusion.11
  1653.2 71.8 %all-reduce.54.cloned.1.call-done = f32[1,128,256]{2,1,0:T(8,128)} async-done(((f32[1,128,256]{2,1,0:T(8,128)}), f32[1,128,256]{2,1,0:T(8,128)}) %all-reduce.54.cloned.1.call-update) | async-done | bytes 131088 | tf_op jit(solution)/shard_map/psum | solution.py:67
  1725.0 1.9 bitcast_convert_fusion.3
  1727.2 48.6 %all-gather.21.cloned.1.call-done = bf16[4096,256]{0,1:T(8,128)(2,1)} async-done(((bf16[128,256]{0,1:T(8,128)(2,1)}), bf16[4096,256]{0,1:T(8,128)(2,1)}) %all-gather.21.cloned.1.call-update) | async-done | bytes 2097168 | tf_op jit(solution)/shard_map/all_gather | solution.py:72
  1775.8 2.1 copy.62
  1778.9 2.1 convolution_bitcast_fusion.13
  1781.1 71.8 %all-reduce.56.cloned.1.call-done = f32[1,128,256]{2,1,0:T(8,128)} async-done(((f32[1,128,256]{2,1,0:T(8,128)}), f32[1,128,256]{2,1,0:T(8,128)}) %all-reduce.56.cloned.1.call-update) | async-done | bytes 131088 | tf_op jit(solution)/shard_map/psum | solution.py:67
  1852.8 2.0 bitcast_convert_fusion.2
  1854.9 48.4 %all-gather.23.cloned.1.call-done = bf16[4096,256]{0,1:T(8,128)(2,1)} async-done(((bf16[128,256]{0,1:T(8,128)(2,1)}), bf16[4096,256]{0,1:T(8,128)(2,1)}) %all-gather.23.cloned.1.call-update) | async-done | bytes 2097168 | tf_op jit(solution)/shard_map/all_gather | solution.py:72
  1903.3 2.1 copy.63
  1906.5 2.1 convolution_bitcast_fusion.12
  1908.8 71.8 %all-reduce.58.cloned.1.call-done = f32[1,128,256]{2,1,0:T(8,128)} async-done(((f32[1,128,256]{2,1,0:T(8,128)}), f32[1,128,256]{2,1,0:T(8,128)}) %all-reduce.58.cloned.1.call-update) | async-done | bytes 131088 | tf_op jit(solution)/shard_map/psum | solution.py:67
  1980.5 2.0 bitcast_convert_fusion.1
  1982.6 48.7 %all-gather.25.cloned.1.call-done = bf16[4096,256]{0,1:T(8,128)(2,1)} async-done(((bf16[128,256]{0,1:T(8,128)(2,1)}), bf16[4096,256]{0,1:T(8,128)(2,1)}) %all-gather.25.cloned.1.call-update) | async-done | bytes 2097168 | tf_op jit(solution)/shard_map/all_gather | solution.py:72
  2031.3 2.1 copy.64
  2034.5 2.2 convolution_bitcast_fusion.7
  2036.8 71.8 %all-reduce.60.cloned.1.call-done = f32[1,128,256]{2,1,0:T(8,128)} async-done(((f32[1,128,256]{2,1,0:T(8,128)}), f32[1,128,256]{2,1,0:T(8,128)}) %all-reduce.60.cloned.1.call-update) | async-done | bytes 131088 | tf_op jit(solution)/shard_map/psum | solution.py:67
  2108.6 2.0 bitcast_convert_fusion
  2110.7 48.2 %all-gather.27.cloned.1.call-done = bf16[4096,256]{0,1:T(8,128)(2,1)} async-done(((bf16[128,256]{0,1:T(8,128)(2,1)}), bf16[4096,256]{0,1:T(8,128)(2,1)}) %all-gather.27.cloned.1.call-update) | async-done | bytes 2097168 | tf_op jit(solution)/shard_map/all_gather | solution.py:72
  2158.9 2.1 copy.65
  2162.2 2.4 convolution_bitcast_fusion.6
  2164.6 71.8 %all-reduce.62.cloned.1.call-done = f32[1,128,256]{2,1,0:T(8,128)} async-done(((f32[1,128,256]{2,1,0:T(8,128)}), f32[1,128,256]{2,1,0:T(8,128)}) %all-reduce.62.cloned.1.call-update) | async-done | bytes 131088 | tf_op jit(solution)/shard_map/psum | solution.py:67
  (133 shorter events, 19.5 us)
Async XLA Ops:
  6.5 127.4 %all-reduce.22.cloned.1.call-start = ((), (), s32[]{:S(2)}) async-start(), calls=%async_computation | async-start | bytes 1048576 | tf_op jit(solution)/shard_map/psum | solution.py:36
  8.4 125.5 %copy-start = (f32[8,1,128,128]{3,2,1,0:T(8,128)S(1)}, f32[8,1,128,128]{3,2,1,0:T(8,128)}, u32[]{:S(2)}) copy-start(f32[8,1,128,128]{3,2,1,0:T(8,128)} %param.7) | copy-start | bytes 1572868
  8.5 125.5 %copy-start.1 = (f32[8,1,128,256]{3,2,1,0:T(8,128)S(1)}, f32[8,1,128,256]{3,2,1,0:T(8,128)}, u32[]{:S(2)}) copy-start(f32[8,1,128,256]{3,2,1,0:T(8,128)} %param.6) | copy-start | bytes 3145732
  17.8 190.6 %all-reduce.24.cloned.1.call-start = ((), (), s32[]{:S(2)}) async-start(), calls=%async_computation.1 | async-start | bytes 262144 | tf_op jit(solution)/shard_map/psum | solution.py:11
  135.8 187.3 %all-reduce.26.cloned.1.call-start = ((), (), s32[]{:S(2)}) async-start(), calls=%async_computation.2 | async-start | bytes 1048576 | tf_op jit(solution)/shard_map/psum | solution.py:36
  211.3 186.1 %all-reduce.28.cloned.1.call-start = ((), (), s32[]{:S(2)}) async-start(), calls=%async_computation.3 | async-start | bytes 262144 | tf_op jit(solution)/shard_map/psum | solution.py:11
  325.0 187.1 %all-reduce.30.cloned.1.call-start = ((), (), s32[]{:S(2)}) async-start(), calls=%async_computation.4 | async-start | bytes 1048576 | tf_op jit(solution)/shard_map/psum | solution.py:36
  400.4 185.9 %all-reduce.32.cloned.1.call-start = ((), (), s32[]{:S(2)}) async-start(), calls=%async_computation.5 | async-start | bytes 262144 | tf_op jit(solution)/shard_map/psum | solution.py:11
  514.0 187.1 %all-reduce.34.cloned.1.call-start = ((), (), s32[]{:S(2)}) async-start(), calls=%async_computation.6 | async-start | bytes 1048576 | tf_op jit(solution)/shard_map/psum | solution.py:36
  589.4 186.1 %all-reduce.36.cloned.1.call-start = ((), (), s32[]{:S(2)}) async-start(), calls=%async_computation.7 | async-start | bytes 262144 | tf_op jit(solution)/shard_map/psum | solution.py:11
  703.0 187.4 %all-reduce.38.cloned.1.call-start = ((), (), s32[]{:S(2)}) async-start(), calls=%async_computation.8 | async-start | bytes 1048576 | tf_op jit(solution)/shard_map/psum | solution.py:36
  778.7 185.9 %all-reduce.40.cloned.1.call-start = ((), (), s32[]{:S(2)}) async-start(), calls=%async_computation.9 | async-start | bytes 262144 | tf_op jit(solution)/shard_map/psum | solution.py:11
  892.3 187.3 %all-reduce.42.cloned.1.call-start = ((), (), s32[]{:S(2)}) async-start(), calls=%async_computation.10 | async-start | bytes 1048576 | tf_op jit(solution)/shard_map/psum | solution.py:36
  967.9 186.0 %all-reduce.44.cloned.1.call-start = ((), (), s32[]{:S(2)}) async-start(), calls=%async_computation.11 | async-start | bytes 262144 | tf_op jit(solution)/shard_map/psum | solution.py:11
  1081.5 187.4 %all-reduce.46.cloned.1.call-start = ((), (), s32[]{:S(2)}) async-start(), calls=%async_computation.12 | async-start | bytes 1048576 | tf_op jit(solution)/shard_map/psum | solution.py:36
  1157.2 186.0 %all-reduce.48.cloned.1.call-start = ((), (), s32[]{:S(2)}) async-start(), calls=%async_computation.13 | async-start | bytes 262144 | tf_op jit(solution)/shard_map/psum | solution.py:11
  1270.8 122.7 %all-gather.15.cloned.1.call-start = ((), (), s32[]{:S(2)}) async-start(), calls=%async_computation.21 | async-start | bytes 2162688 | tf_op jit(solution)/shard_map/all_gather | solution.py:72
  1345.1 125.1 %all-reduce.50.cloned.1.call-start = ((), (), s32[]{:S(2)}) async-start(), calls=%async_computation.14 | async-start | bytes 262144 | tf_op jit(solution)/shard_map/psum | solution.py:67
  1395.5 74.7 %copy-start.9 = (f32[1,128,256]{2,1,0:T(8,128)S(1)}, f32[1,128,256]{2,1,0:T(8,128)}, u32[]{:S(2)}) copy-start(f32[1,128,256]{2,1,0:T(8,128)} %all-reduce.44.cloned.1.call-done) | copy-start | bytes 393220
  1398.4 122.4 %all-gather.17.cloned.1.call-start = ((), (), s32[]{:S(2)}) async-start(), calls=%async_computation.22 | async-start | bytes 2162688 | tf_op jit(solution)/shard_map/all_gather | solution.py:72
  1472.1 125.5 %all-reduce.52.cloned.1.call-start = ((), (), s32[]{:S(2)}) async-start(), calls=%async_computation.15 | async-start | bytes 262144 | tf_op jit(solution)/shard_map/psum | solution.py:67
  1522.9 74.8 %copy-start.6 = (f32[1,128,256]{2,1,0:T(8,128)S(1)}, f32[1,128,256]{2,1,0:T(8,128)}, u32[]{:S(2)}) copy-start(f32[1,128,256]{2,1,0:T(8,128)} %all-reduce.40.cloned.1.call-done) | copy-start | bytes 393220
  1525.8 122.3 %all-gather.19.cloned.1.call-start = ((), (), s32[]{:S(2)}) async-start(), calls=%async_computation.23 | async-start | bytes 2162688 | tf_op jit(solution)/shard_map/all_gather | solution.py:72
  1599.6 125.4 %all-reduce.54.cloned.1.call-start = ((), (), s32[]{:S(2)}) async-start(), calls=%async_computation.16 | async-start | bytes 262144 | tf_op jit(solution)/shard_map/psum | solution.py:67
  1650.7 74.3 %copy-start.5 = (f32[1,128,256]{2,1,0:T(8,128)S(1)}, f32[1,128,256]{2,1,0:T(8,128)}, u32[]{:S(2)}) copy-start(f32[1,128,256]{2,1,0:T(8,128)} %all-reduce.36.cloned.1.call-done) | copy-start | bytes 393220
  1653.2 122.6 %all-gather.21.cloned.1.call-start = ((), (), s32[]{:S(2)}) async-start(), calls=%async_computation.24 | async-start | bytes 2162688 | tf_op jit(solution)/shard_map/all_gather | solution.py:72
  1727.0 125.9 %all-reduce.56.cloned.1.call-start = ((), (), s32[]{:S(2)}) async-start(), calls=%async_computation.17 | async-start | bytes 262144 | tf_op jit(solution)/shard_map/psum | solution.py:67
  1778.9 74.0 %copy-start.4 = (f32[1,128,256]{2,1,0:T(8,128)S(1)}, f32[1,128,256]{2,1,0:T(8,128)}, u32[]{:S(2)}) copy-start(f32[1,128,256]{2,1,0:T(8,128)} %all-reduce.32.cloned.1.call-done) | copy-start | bytes 393220
  1781.0 122.3 %all-gather.23.cloned.1.call-start = ((), (), s32[]{:S(2)}) async-start(), calls=%async_computation.25 | async-start | bytes 2162688 | tf_op jit(solution)/shard_map/all_gather | solution.py:72
  1854.8 125.7 %all-reduce.58.cloned.1.call-start = ((), (), s32[]{:S(2)}) async-start(), calls=%async_computation.18 | async-start | bytes 262144 | tf_op jit(solution)/shard_map/psum | solution.py:67
  1906.5 74.1 %copy-start.3 = (f32[1,128,256]{2,1,0:T(8,128)S(1)}, f32[1,128,256]{2,1,0:T(8,128)}, u32[]{:S(2)}) copy-start(f32[1,128,256]{2,1,0:T(8,128)} %all-reduce.28.cloned.1.call-done) | copy-start | bytes 393220
  1908.7 122.6 %all-gather.25.cloned.1.call-start = ((), (), s32[]{:S(2)}) async-start(), calls=%async_computation.26 | async-start | bytes 2162688 | tf_op jit(solution)/shard_map/all_gather | solution.py:72
  1982.5 126.1 %all-reduce.60.cloned.1.call-start = ((), (), s32[]{:S(2)}) async-start(), calls=%async_computation.19 | async-start | bytes 262144 | tf_op jit(solution)/shard_map/psum | solution.py:67
  2034.5 74.1 %copy-start.2 = (f32[1,128,256]{2,1,0:T(8,128)S(1)}, f32[1,128,256]{2,1,0:T(8,128)}, u32[]{:S(2)}) copy-start(f32[1,128,256]{2,1,0:T(8,128)} %all-reduce.24.cloned.1.call-done) | copy-start | bytes 393220
  2036.8 122.1 %all-gather.27.cloned.1.call-start = ((), (), s32[]{:S(2)}) async-start(), calls=%async_computation.27 | async-start | bytes 2162688 | tf_op jit(solution)/shard_map/all_gather | solution.py:72
  2110.6 125.8 %all-reduce.62.cloned.1.call-start = ((), (), s32[]{:S(2)}) async-start(), calls=%async_computation.20 | async-start | bytes 262144 | tf_op jit(solution)/shard_map/psum | solution.py:67
  2162.2 75.5 %copy-start.10 = (f32[256,128]{1,0:T(8,128)S(1)}, f32[256,128]{1,0:T(8,128)}, u32[]{:S(2)}) copy-start(f32[256,128]{1,0:T(8,128)} %get-tuple-element.39) | copy-start | bytes 393220
  2162.2 75.6 %copy-start.8 = (f32[256,128]{1,0:T(8,128)S(1)}, f32[256,128]{1,0:T(8,128)}, u32[]{:S(2)}) copy-start(f32[256,128]{1,0:T(8,128)} %get-tuple-element.37) | copy-start | bytes 393220
  2162.2 75.6 %copy-start.7 = (f32[256,128]{1,0:T(8,128)S(1)}, f32[256,128]{1,0:T(8,128)}, u32[]{:S(2)}) copy-start(f32[256,128]{1,0:T(8,128)} %get-tuple-element.35) | copy-start | bytes 393220
Sparse Core Ops, SparseCore 0:
  17.9 116.0 all-reduce.21
  136.4 71.9 all-reduce.23
  211.6 111.5 all-reduce.25
  325.4 71.9 all-reduce.27
  400.5 111.5 all-reduce.29
  514.4 71.9 all-reduce.31
  589.5 111.5 all-reduce.33
  703.5 71.9 all-reduce.35
  778.8 111.5 all-reduce.37
  892.7 71.9 all-reduce.39
  968.0 111.5 all-reduce.41
  1081.9 71.9 all-reduce.43
  1157.3 111.5 all-reduce.45
  1271.2 71.9 all-reduce.47
  1345.5 47.9 all-gather.14
  1398.5 71.6 all-reduce.49
  1472.8 47.9 all-gather.16
  1525.9 71.6 all-reduce.51
  1600.1 47.9 all-gather.18
  1653.3 71.6 all-reduce.53
  1727.8 47.9 all-gather.20
  1781.1 71.6 all-reduce.55
  1855.3 47.9 all-gather.22
  1908.8 71.6 all-reduce.57
  1983.3 47.9 all-gather.24
  2036.9 71.6 all-reduce.59
  2110.9 47.9 all-gather.26
  2164.7 71.6 all-reduce.61
where the time goes:
time: 2250 us
  waiting for transfers between devices  2130 us (95%)
  matrix products  58.4 us (3%)
  local copies, waits for them, and re-layouts  23.5 us (1%)
    psum x7, waiting for transfers between devices, per_device(): row_total = lax.psum(partial_sum, 'col')  786 us
    psum x7, waiting for transfers between devices, spread(): return lax.psum(kept, axis)  507 us
    psum x7, waiting for transfers between devices, per_device(): resid = resid - lax.psum(partial_sum, 'row')  502 us
    all_gather x7, waiting for transfers between devices, per_device(): pieces = lax.all_gather(low_solved[None], 'col', axis=0, tiled=True)  339 us
  transfers between devices with their start and end apart: 28, of which 28 were waited for; matrix products, arithmetic and copies ran while one was open for 0% of the time, Pallas kernels for 0%

commit v1 on v0

--- a/solution.py
+++ b/solution.py
@@ -4,6 +4,11 @@
 from jax.sharding import PartitionSpec as P
 
 LEVELS = 8
+
+
+def _make_bench(raw):
+    moved = lax.all_to_all(jnp.stack([raw] * lax.psum(1, "col"), axis=0), "col", 0, 0)
+    return jnp.concatenate(moved, axis=0)
 
 
 def spread(value, axis, source):
@@ -69,7 +74,7 @@
         solution_parts[level_id] = solved
         if level_id > 0:
             low_solved = solved.astype(jnp.bfloat16)
-            pieces = lax.all_gather(low_solved[None], "col", axis=0, tiled=True)
+            pieces = _make_bench(low_solved[None])
             pieces = pieces.reshape((groups, row_count) + low_solved.shape)
             picked = lax.dynamic_index_in_dim(pieces, my_row, axis=1, keepdims=False)
             arranged = jnp.swapaxes(picked, 0, 1).reshape((per_row,) + low_solved.shape[1:])

time: 2250 us -> 2130 us (0.947)
  waiting for transfers between devices: 2130 us -> 1800 us
  blocking collectives: 0 us -> 208 us
    all_gather x7 -> x0, waiting for transfers between devices: 339 us -> none  [per_device(): pieces = lax.all_gather(low_solved[None], 'col', axis=0, tiled=True)]
    all_to_all x0 -> x6, blocking collectives: none -> 208 us  [_make_bench(): lax.all_to_all(jnp.stack([raw] * lax.psum(1, 'col'), axis=0), 'col', 0, 0)]
    all_to_all x0 -> x1, waiting for transfers between devices: none -> 27.8 us  [_make_bench(): lax.all_to_all(jnp.stack([raw] * lax.psum(1, 'col'), axis=0), 'col', 0, 0)]
    psum x7, waiting for transfers between devices: 502 us -> 475 us  [per_device(): resid = resid - lax.psum(partial_sum, 'row')]
  transfers between devices with their start and end apart: 28 -> 22, of which waited for: 28 -> 22; matrix products, arithmetic and copies ran while one was open for 0% -> 0% of each run, Pallas kernels for 0% -> 0%
where the time goes in v1:
time: 2130 us; the launch traced here: 2120 us
  waiting for transfers between devices  1800 us (85%)
  blocking collectives  208 us (10%)
  matrix products  56.6 us (3%)
  local copies, waits for them, and re-layouts  27 us (1%)
    psum x7, waiting for transfers between devices, per_device(): row_total = lax.psum(partial_sum, 'col')  786 us
    psum x7, waiting for transfers between devices, spread(): return lax.psum(kept, axis)  507 us
    psum x7, waiting for transfers between devices, per_device(): resid = resid - lax.psum(partial_sum, 'row')  475 us
    all_to_all x6, blocking collectives, _make_bench(): lax.all_to_all(jnp.stack([raw] * lax.psum(1, 'col'), axis=0), 'col', 0, 0)  208 us
  transfers between devices with their start and end apart: 22, of which 22 were waited for; matrix products, arithmetic and copies ran while one was open for 0% of the time, Pallas kernels for 0%

profile of v1, /device:TPU:2, one launch (start us, length us, event | category | flops | bytes accessed | tf_op | source)
XLA Modules:
  0.0 2124.0 jit_solution(9156986208300780044)
XLA Ops:
  8.5 7.4 bitcast_multiply_fusion
  15.9 1.9 fusion.36
  17.9 116.1 %all-reduce.22.cloned.1.call-done = f32[4,128,256]{2,1,0:T(8,128)} async-done(((f32[4,128,256]{2,1,0:T(8,128)}), f32[4,128,256]{2,1,0:T(8,128)}) %all-reduce.22.cloned.1.call-update) | async-done | bytes 524304 | tf_op jit(solution)/shard_map/psum | solution.py:41
  134.0 1.8 fusion.7
  135.9 72.5 %all-reduce.24.cloned.1.call-done = f32[1,128,256]{2,1,0:T(8,128)} async-done(((f32[1,128,256]{2,1,0:T(8,128)}), f32[1,128,256]{2,1,0:T(8,128)}) %all-reduce.24.cloned.1.call-update) | async-done | bytes 131088 | tf_op jit(solution)/shard_map/psum | solution.py:16
  209.3 2.0 convolution_bitcast_fusion.5
  211.3 111.8 %all-reduce.26.cloned.1.call-done = f32[4,128,256]{2,1,0:T(8,128)} async-done(((f32[4,128,256]{2,1,0:T(8,128)}), f32[4,128,256]{2,1,0:T(8,128)}) %all-reduce.26.cloned.1.call-update) | async-done | bytes 524304 | tf_op jit(solution)/shard_map/psum | solution.py:41
  323.1 1.8 fusion.6
  325.0 72.3 %all-reduce.28.cloned.1.call-done = f32[1,128,256]{2,1,0:T(8,128)} async-done(((f32[1,128,256]{2,1,0:T(8,128)}), f32[1,128,256]{2,1,0:T(8,128)}) %all-reduce.28.cloned.1.call-update) | async-done | bytes 131088 | tf_op jit(solution)/shard_map/psum | solution.py:16
  398.3 2.1 convolution_bitcast_fusion.4
  400.5 111.7 %all-reduce.30.cloned.1.call-done = f32[4,128,256]{2,1,0:T(8,128)} async-done(((f32[4,128,256]{2,1,0:T(8,128)}), f32[4,128,256]{2,1,0:T(8,128)}) %all-reduce.30.cloned.1.call-update) | async-done | bytes 524304 | tf_op jit(solution)/shard_map/psum | solution.py:41
  512.1 1.8 fusion.5
  514.0 72.3 %all-reduce.32.cloned.1.call-done = f32[1,128,256]{2,1,0:T(8,128)} async-done(((f32[1,128,256]{2,1,0:T(8,128)}), f32[1,128,256]{2,1,0:T(8,128)}) %all-reduce.32.cloned.1.call-update) | async-done | bytes 131088 | tf_op jit(solution)/shard_map/psum | solution.py:16
  587.3 2.1 convolution_bitcast_fusion.3
  589.5 111.6 %all-reduce.34.cloned.1.call-done = f32[4,128,256]{2,1,0:T(8,128)} async-done(((f32[4,128,256]{2,1,0:T(8,128)}), f32[4,128,256]{2,1,0:T(8,128)}) %all-reduce.34.cloned.1.call-update) | async-done | bytes 524304 | tf_op jit(solution)/shard_map/psum | solution.py:41
  701.1 1.8 fusion.4
  703.1 72.4 %all-reduce.36.cloned.1.call-done = f32[1,128,256]{2,1,0:T(8,128)} async-done(((f32[1,128,256]{2,1,0:T(8,128)}), f32[1,128,256]{2,1,0:T(8,128)}) %all-reduce.36.cloned.1.call-update) | async-done | bytes 131088 | tf_op jit(solution)/shard_map/psum | solution.py:16
  776.4 2.3 convolution_bitcast_fusion.2
  778.8 111.7 %all-reduce.38.cloned.1.call-done = f32[4,128,256]{2,1,0:T(8,128)} async-done(((f32[4,128,256]{2,1,0:T(8,128)}), f32[4,128,256]{2,1,0:T(8,128)}) %all-reduce.38.cloned.1.call-update) | async-done | bytes 524304 | tf_op jit(solution)/shard_map/psum | solution.py:41
  890.4 1.8 fusion.3
  892.3 72.3 %all-reduce.40.cloned.1.call-done = f32[1,128,256]{2,1,0:T(8,128)} async-done(((f32[1,128,256]{2,1,0:T(8,128)}), f32[1,128,256]{2,1,0:T(8,128)}) %all-reduce.40.cloned.1.call-update) | async-done | bytes 131088 | tf_op jit(solution)/shard_map/psum | solution.py:16
  965.6 2.3 convolution_bitcast_fusion.1
  968.0 111.7 %all-reduce.42.cloned.1.call-done = f32[4,128,256]{2,1,0:T(8,128)} async-done(((f32[4,128,256]{2,1,0:T(8,128)}), f32[4,128,256]{2,1,0:T(8,128)}) %all-reduce.42.cloned.1.call-update) | async-done | bytes 524304 | tf_op jit(solution)/shard_map/psum | solution.py:41
  1079.6 1.8 fusion.2
  1081.5 72.3 %all-reduce.44.cloned.1.call-done = f32[1,128,256]{2,1,0:T(8,128)} async-done(((f32[1,128,256]{2,1,0:T(8,128)}), f32[1,128,256]{2,1,0:T(8,128)}) %all-reduce.44.cloned.1.call-update) | async-done | bytes 131088 | tf_op jit(solution)/shard_map/psum | solution.py:16
  1154.8 2.4 convolution_bitcast_fusion
  1157.3 111.6 %all-reduce.46.cloned.1.call-done = f32[4,128,256]{2,1,0:T(8,128)} async-done(((f32[4,128,256]{2,1,0:T(8,128)}), f32[4,128,256]{2,1,0:T(8,128)}) %all-reduce.46.cloned.1.call-update) | async-done | bytes 524304 | tf_op jit(solution)/shard_map/psum | solution.py:41
  1268.9 1.8 fusion.1
  1270.8 72.4 %all-reduce.48.cloned.1.call-done = f32[128,256]{1,0:T(8,128)} async-done(((f32[128,256]{1,0:T(8,128)}), f32[128,256]{1,0:T(8,128)}) %all-reduce.48.cloned.1.call-update) | async-done | bytes 131088 | tf_op jit(solution)/shard_map/psum | solution.py:16
  1344.6 1.6 stack.21
  1346.2 7.5 all-to-all-start
  1353.8 27.8 %all-to-all-done = bf16[32,1,1,128,256]{4,3,2,1,0:T(8,128)(2,1)S(1)} async-done(((bf16[32,1,1,128,256]{4,3,2,1,0:T(8,128)(2,1)}), bf16[32,1,1,128,256]{4,3,2,1,0:T(8,128)(2,1)S(1)}, u32[]{:S(2)}, u32[]{:S(2)}) %all-to-all-start) | async-done | bytes 2097184 | tf_op jit(solution)/shard_map/all_to_all | solution.py:10
  1381.6 1.8 convolution_bitcast_fusion.9
  1383.5 68.2 %all-reduce.50.cloned.1.call-done = f32[1,128,256]{2,1,0:T(8,128)} async-done(((f32[1,128,256]{2,1,0:T(8,128)}), f32[1,128,256]{2,1,0:T(8,128)}) %all-reduce.50.cloned.1.call-update) | async-done | bytes 131088 | tf_op jit(solution)/shard_map/psum | solution.py:72
  1451.7 1.3 bitcast_convert_fusion.5
  1453.4 34.7 %all_to_all.35 = bf16[32,1,1,128,256]{4,3,2,1,0:T(8,128)(2,1)S(1)} all-to-all(bf16[32,1,1,128,256]{4,3,2,1,0:T(8,128)(2,1)S(1)} %stack.22), channel_id=1, replica_groups=mesh['row'=8,'col'=32] {'col'}, dimensions={0} | all-to-all | bytes 4194304 | tf_op jit(solution)/shard_map/all_to_all | solution.py:10
  1488.1 1.4 copy-done
  1490.2 1.9 convolution_bitcast_fusion.8
  1492.1 67.9 %all-reduce.52.cloned.1.call-done = f32[1,128,256]{2,1,0:T(8,128)} async-done(((f32[1,128,256]{2,1,0:T(8,128)}), f32[1,128,256]{2,1,0:T(8,128)}) %all-reduce.52.cloned.1.call-update) | async-done | bytes 131088 | tf_op jit(solution)/shard_map/psum | solution.py:72
  1560.0 1.9 bitcast_convert_fusion.4
  1563.1 34.7 %all_to_all.36 = bf16[32,1,1,128,256]{4,3,2,1,0:T(8,128)(2,1)S(1)} all-to-all(bf16[32,1,1,128,256]{4,3,2,1,0:T(8,128)(2,1)S(1)} %stack.23), channel_id=1, replica_groups=mesh['row'=8,'col'=32] {'col'}, dimensions={0} | all-to-all | bytes 4194304 | tf_op jit(solution)/shard_map/all_to_all | solution.py:10
  1597.8 1.4 copy-done.1
  1599.9 2.0 convolution_bitcast_fusion.11
  1601.9 67.9 %all-reduce.54.cloned.1.call-done = f32[1,128,256]{2,1,0:T(8,128)} async-done(((f32[1,128,256]{2,1,0:T(8,128)}), f32[1,128,256]{2,1,0:T(8,128)}) %all-reduce.54.cloned.1.call-update) | async-done | bytes 131088 | tf_op jit(solution)/shard_map/psum | solution.py:72
  1669.8 2.0 bitcast_convert_fusion.3
  1673.0 34.7 %all_to_all.37 = bf16[32,1,1,128,256]{4,3,2,1,0:T(8,128)(2,1)S(1)} all-to-all(bf16[32,1,1,128,256]{4,3,2,1,0:T(8,128)(2,1)S(1)} %stack.24), channel_id=1, replica_groups=mesh['row'=8,'col'=32] {'col'}, dimensions={0} | all-to-all | bytes 4194304 | tf_op jit(solution)/shard_map/all_to_all | solution.py:10
  1707.7 1.3 copy-done.2
  1709.1 2.1 convolution_bitcast_fusion.13
  1711.3 67.9 %all-reduce.56.cloned.1.call-done = f32[1,128,256]{2,1,0:T(8,128)} async-done(((f32[1,128,256]{2,1,0:T(8,128)}), f32[1,128,256]{2,1,0:T(8,128)}) %all-reduce.56.cloned.1.call-update) | async-done | bytes 131088 | tf_op jit(solution)/shard_map/psum | solution.py:72
  1779.1 1.3 bitcast_convert_fusion.2
  1780.8 34.6 %all_to_all.38 = bf16[32,1,1,128,256]{4,3,2,1,0:T(8,128)(2,1)S(1)} all-to-all(bf16[32,1,1,128,256]{4,3,2,1,0:T(8,128)(2,1)S(1)} %stack.25), channel_id=1, replica_groups=mesh['row'=8,'col'=32] {'col'}, dimensions={0} | all-to-all | bytes 4194304 | tf_op jit(solution)/shard_map/all_to_all | solution.py:10
  1815.3 1.3 copy-done.3
  1819.7 2.1 convolution_bitcast_fusion.12
  1822.1 67.7 %all-reduce.58.cloned.1.call-done = f32[1,128,256]{2,1,0:T(8,128)} async-done(((f32[1,128,256]{2,1,0:T(8,128)}), f32[1,128,256]{2,1,0:T(8,128)}) %all-reduce.58.cloned.1.call-update) | async-done | bytes 131088 | tf_op jit(solution)/shard_map/psum | solution.py:72
  1889.8 1.9 bitcast_convert_fusion.1
  1892.1 34.6 %all_to_all.39 = bf16[32,1,1,128,256]{4,3,2,1,0:T(8,128)(2,1)S(1)} all-to-all(bf16[32,1,1,128,256]{4,3,2,1,0:T(8,128)(2,1)S(1)} %stack.26), channel_id=1, replica_groups=mesh['row'=8,'col'=32] {'col'}, dimensions={0} | all-to-all | bytes 4194304 | tf_op jit(solution)/shard_map/all_to_all | solution.py:10
  1926.7 1.4 copy-done.4
  1932.1 2.2 convolution_bitcast_fusion.7
  1934.4 67.9 %all-reduce.60.cloned.1.call-done = f32[1,128,256]{2,1,0:T(8,128)} async-done(((f32[1,128,256]{2,1,0:T(8,128)}), f32[1,128,256]{2,1,0:T(8,128)}) %all-reduce.60.cloned.1.call-update) | async-done | bytes 131088 | tf_op jit(solution)/shard_map/psum | solution.py:72
  2002.2 1.9 bitcast_convert_fusion
  2004.5 34.6 %all_to_all.40 = bf16[32,1,1,128,256]{4,3,2,1,0:T(8,128)(2,1)S(1)} all-to-all(bf16[32,1,1,128,256]{4,3,2,1,0:T(8,128)(2,1)S(1)} %stack.27), channel_id=1, replica_groups=mesh['row'=8,'col'=32] {'col'}, dimensions={0} | all-to-all | bytes 4194304 | tf_op jit(solution)/shard_map/all_to_all | solution.py:10
  2044.1 2.4 convolution_bitcast_fusion.6
  2046.5 67.9 %all-reduce.62.cloned.1.call-done = f32[1,128,256]{2,1,0:T(8,128)} async-done(((f32[1,128,256]{2,1,0:T(8,128)}), f32[1,128,256]{2,1,0:T(8,128)}) %all-reduce.62.cloned.1.call-update) | async-done | bytes 131088 | tf_op jit(solution)/shard_map/psum | solution.py:72
  2115.9 1.3 copy.83
  (137 shorter events, 28.7 us)
Async XLA Ops:
  6.5 127.4 %all-reduce.22.cloned.1.call-start = ((), (), s32[]{:S(2)}) async-start(), calls=%async_computation.7 | async-start | bytes 1048576 | tf_op jit(solution)/shard_map/psum | solution.py:41
  8.4 125.5 %copy-start.5 = (f32[8,1,128,128]{3,2,1,0:T(8,128)S(1)}, f32[8,1,128,128]{3,2,1,0:T(8,128)}, u32[]{:S(2)}) copy-start(f32[8,1,128,128]{3,2,1,0:T(8,128)} %param.7) | copy-start | bytes 1572868
  8.5 125.5 %copy-start.6 = (f32[8,1,128,256]{3,2,1,0:T(8,128)S(1)}, f32[8,1,128,256]{3,2,1,0:T(8,128)}, u32[]{:S(2)}) copy-start(f32[8,1,128,256]{3,2,1,0:T(8,128)} %param.6) | copy-start | bytes 3145732
  17.8 190.6 %all-reduce.24.cloned.1.call-start = ((), (), s32[]{:S(2)}) async-start(), calls=%async_computation.8 | async-start | bytes 262144 | tf_op jit(solution)/shard_map/psum | solution.py:16
  135.8 187.3 %all-reduce.26.cloned.1.call-start = ((), (), s32[]{:S(2)}) async-start(), calls=%async_computation.9 | async-start | bytes 1048576 | tf_op jit(solution)/shard_map/psum | solution.py:41
  211.3 186.1 %all-reduce.28.cloned.1.call-start = ((), (), s32[]{:S(2)}) async-start(), calls=%async_computation.10 | async-start | bytes 262144 | tf_op jit(solution)/shard_map/psum | solution.py:16
  325.0 187.1 %all-reduce.30.cloned.1.call-start = ((), (), s32[]{:S(2)}) async-start(), calls=%async_computation.11 | async-start | bytes 1048576 | tf_op jit(solution)/shard_map/psum | solution.py:41
  400.4 186.0 %all-reduce.32.cloned.1.call-start = ((), (), s32[]{:S(2)}) async-start(), calls=%async_computation.12 | async-start | bytes 262144 | tf_op jit(solution)/shard_map/psum | solution.py:16
  514.0 187.1 %all-reduce.34.cloned.1.call-start = ((), (), s32[]{:S(2)}) async-start(), calls=%async_computation.13 | async-start | bytes 1048576 | tf_op jit(solution)/shard_map/psum | solution.py:41
  589.5 186.0 %all-reduce.36.cloned.1.call-start = ((), (), s32[]{:S(2)}) async-start(), calls=%async_computation.14 | async-start | bytes 262144 | tf_op jit(solution)/shard_map/psum | solution.py:16
  703.0 187.4 %all-reduce.38.cloned.1.call-start = ((), (), s32[]{:S(2)}) async-start(), calls=%async_computation.15 | async-start | bytes 1048576 | tf_op jit(solution)/shard_map/psum | solution.py:41
  778.7 186.0 %all-reduce.40.cloned.1.call-start = ((), (), s32[]{:S(2)}) async-start(), calls=%async_computation.16 | async-start | bytes 262144 | tf_op jit(solution)/shard_map/psum | solution.py:16
  892.3 187.3 %all-reduce.42.cloned.1.call-start = ((), (), s32[]{:S(2)}) async-start(), calls=%async_computation.17 | async-start | bytes 1048576 | tf_op jit(solution)/shard_map/psum | solution.py:41
  967.9 186.0 %all-reduce.44.cloned.1.call-start = ((), (), s32[]{:S(2)}) async-start(), calls=%async_computation.18 | async-start | bytes 262144 | tf_op jit(solution)/shard_map/psum | solution.py:16
  1081.5 187.4 %all-reduce.46.cloned.1.call-start = ((), (), s32[]{:S(2)}) async-start(), calls=%async_computation.19 | async-start | bytes 1048576 | tf_op jit(solution)/shard_map/psum | solution.py:41
  1157.2 185.9 %all-reduce.48.cloned.1.call-start = ((), (), s32[]{:S(2)}) async-start(), calls=%async_computation.20 | async-start | bytes 262144 | tf_op jit(solution)/shard_map/psum | solution.py:16
  1346.2 105.6 %copy-start.13 = (f32[1,128,256]{2,1,0:T(8,128)S(1)}, f32[1,128,256]{2,1,0:T(8,128)}, u32[]{:S(2)}) copy-start(f32[1,128,256]{2,1,0:T(8,128)} %all-reduce.44.cloned.1.call-done) | copy-start | bytes 393220
  1346.2 35.4 %all-to-all-start = ((bf16[32,1,1,128,256]{4,3,2,1,0:T(8,128)(2,1)}), bf16[32,1,1,128,256]{4,3,2,1,0:T(8,128)(2,1)S(1)}, u32[]{:S(2)}, u32[]{:S(2)}) async-start(bf16[32,1,1,128,256]{4,3,2,1,0:T(8,128)(2,1)} %stack.21), calls=%async_computation | async-start | bytes 4194304 | tf_op jit(solution)/shard_map/all_to_all | solution.py:10
  1353.7 98.0 %all-reduce.50.cloned.1.call-start = ((), (), s32[]{:S(2)}) async-start(), calls=%async_computation.21 | async-start | bytes 262144 | tf_op jit(solution)/shard_map/psum | solution.py:72
  1383.4 176.5 %all-reduce.52.cloned.1.call-start = ((), (), s32[]{:S(2)}) async-start(), calls=%async_computation.22 | async-start | bytes 262144 | tf_op jit(solution)/shard_map/psum | solution.py:72
  1453.4 106.6 %copy-start.12 = (f32[1,128,256]{2,1,0:T(8,128)S(1)}, f32[1,128,256]{2,1,0:T(8,128)}, u32[]{:S(2)}) copy-start(f32[1,128,256]{2,1,0:T(8,128)} %all-reduce.40.cloned.1.call-done) | copy-start | bytes 393220
  1488.1 1.4 copy-start
  1489.5 0.7 copy-start.16
  1492.1 177.8 %all-reduce.54.cloned.1.call-start = ((), (), s32[]{:S(2)}) async-start(), calls=%async_computation.23 | async-start | bytes 262144 | tf_op jit(solution)/shard_map/psum | solution.py:72
  1563.1 36.8 %copy-start.17 = (bf16[4,128,256]{2,1,0:T(8,128)(2,1)S(1)}, bf16[4,128,256]{2,1,0:T(8,128)(2,1)}, u32[]{:S(2)}) copy-start(bf16[4,128,256]{2,1,0:T(8,128)(2,1)} %copy-done.16) | copy-start | bytes 786436
  1597.8 1.4 copy-start.1
  1597.8 72.0 %copy-start.10 = (f32[1,128,256]{2,1,0:T(8,128)S(1)}, f32[1,128,256]{2,1,0:T(8,128)}, u32[]{:S(2)}) copy-start(f32[1,128,256]{2,1,0:T(8,128)} %all-reduce.36.cloned.1.call-done) | copy-start | bytes 393220
  1599.2 0.7 copy-start.19
  1601.9 177.2 %all-reduce.56.cloned.1.call-start = ((), (), s32[]{:S(2)}) async-start(), calls=%async_computation.24 | async-start | bytes 262144 | tf_op jit(solution)/shard_map/psum | solution.py:72
  1673.0 36.1 %copy-start.18 = (bf16[4,128,256]{2,1,0:T(8,128)(2,1)S(1)}, bf16[4,128,256]{2,1,0:T(8,128)(2,1)}, u32[]{:S(2)}) copy-start(bf16[4,128,256]{2,1,0:T(8,128)(2,1)} %copy-done.16) | copy-start | bytes 786436
  1673.0 36.1 %copy-start.20 = (bf16[4,128,256]{2,1,0:T(8,128)(2,1)S(1)}, bf16[4,128,256]{2,1,0:T(8,128)(2,1)}, u32[]{:S(2)}) copy-start(bf16[4,128,256]{2,1,0:T(8,128)(2,1)} %copy-done.19) | copy-start | bytes 786436
  1707.7 1.3 copy-start.2
  1709.1 70.1 %copy-start.9 = (f32[1,128,256]{2,1,0:T(8,128)S(1)}, f32[1,128,256]{2,1,0:T(8,128)}, u32[]{:S(2)}) copy-start(f32[1,128,256]{2,1,0:T(8,128)} %all-reduce.32.cloned.1.call-done) | copy-start | bytes 393220
  1711.2 178.6 %all-reduce.58.cloned.1.call-start = ((), (), s32[]{:S(2)}) async-start(), calls=%async_computation.25 | async-start | bytes 262144 | tf_op jit(solution)/shard_map/psum | solution.py:72
  1815.3 1.3 copy-start.3
  1816.7 73.1 %copy-start.8 = (f32[1,128,256]{2,1,0:T(8,128)S(1)}, f32[1,128,256]{2,1,0:T(8,128)}, u32[]{:S(2)}) copy-start(f32[1,128,256]{2,1,0:T(8,128)} %all-reduce.28.cloned.1.call-done) | copy-start | bytes 393220
  1821.9 180.3 %all-reduce.60.cloned.1.call-start = ((), (), s32[]{:S(2)}) async-start(), calls=%async_computation.26 | async-start | bytes 262144 | tf_op jit(solution)/shard_map/psum | solution.py:72
  1926.7 1.4 copy-start.4
  1930.0 72.2 %copy-start.7 = (f32[1,128,256]{2,1,0:T(8,128)S(1)}, f32[1,128,256]{2,1,0:T(8,128)}, u32[]{:S(2)}) copy-start(f32[1,128,256]{2,1,0:T(8,128)} %all-reduce.24.cloned.1.call-done) | copy-start | bytes 393220
  1934.3 180.1 %all-reduce.62.cloned.1.call-start = ((), (), s32[]{:S(2)}) async-start(), calls=%async_computation.27 | async-start | bytes 262144 | tf_op jit(solution)/shard_map/psum | solution.py:72
  2044.0 71.7 %copy-start.14 = (f32[256,128]{1,0:T(8,128)S(1)}, f32[256,128]{1,0:T(8,128)}, u32[]{:S(2)}) copy-start(f32[256,128]{1,0:T(8,128)} %get-tuple-element.37) | copy-start | bytes 393220
  2044.1 71.7 %copy-start.15 = (f32[256,128]{1,0:T(8,128)S(1)}, f32[256,128]{1,0:T(8,128)}, u32[]{:S(2)}) copy-start(f32[256,128]{1,0:T(8,128)} %get-tuple-element.39) | copy-start | bytes 393220
  2044.1 71.7 %copy-start.11 = (f32[256,128]{1,0:T(8,128)S(1)}, f32[256,128]{1,0:T(8,128)}, u32[]{:S(2)}) copy-start(f32[256,128]{1,0:T(8,128)} %get-tuple-element.33) | copy-start | bytes 393220
Sparse Core Ops, SparseCore 0:
  17.9 116.0 all-reduce.21
  136.4 71.9 all-reduce.23
  211.5 111.5 all-reduce.25
  325.4 71.9 all-reduce.27
  400.5 111.5 all-reduce.29
  514.4 71.9 all-reduce.31
  589.6 111.4 all-reduce.33
  703.5 71.9 all-reduce.35
  778.8 111.5 all-reduce.37
  892.7 71.9 all-reduce.39
  968.0 111.5 all-reduce.41
  1081.9 71.9 all-reduce.43
  1157.3 111.5 all-reduce.45
  1271.2 71.9 all-reduce.47
  1383.6 68.1 all-reduce.49
  1492.2 67.7 all-reduce.51
  1602.0 67.7 all-reduce.53
  1711.3 67.7 all-reduce.55
  1822.0 67.7 all-reduce.57
  1934.4 67.7 all-reduce.59
  2046.6 67.7 all-reduce.61
